TPU v7x, 128 devices: a whole 4x4x4 slice. The times are simulated.
128 devices in a mesh: ctx: 8 (over x, y_lo), tp: 8 (over z, core), dp: 2 (over y_hi).
Axes of the slice: x: 4, y: 4 (y_hi: 2, y_lo: 2; y = y_hi * 2 + y_lo), z: 4, core: 2. Of those that a mesh axis runs over, the one named last changes fastest.
Arguments:
- tokens: bfloat16 [16384, 8192], P(('dp', 'ctx', 'tp')), parts along dimension 0, may hold values from -6 to 6
- norm_gain: float32 [8192], replicated, may hold values from 0.1 to 1.9
- w_qkv: bfloat16 [8192, 6144], P(None, 'tp')
- w_out: bfloat16 [4096, 8192], P('tp'), may hold values from -0.75 to 0.75
- doc_lengths: int32 [32], P('dp'), parts along dimension 0, may hold values from 1 to 2048, 8192 in all
- span_slots: int32 [32], P('dp'), parts along dimension 0, may hold values from 0 to 15, as said below
Outputs:
- attn_out: bfloat16 [16384, 8192], P(('dp', 'ctx', 'tp')), parts along dimension 0
There are 2 independent parts, one for each index of `dp`. A program takes and returns all parts, laid end to end along the dimension named above; an argument that names none is the same for every part. Nothing has to cross between parts.
Inputs may be any that keep to these rules, and one draw needn't show every extreme that they name: `span_slots`: every position block appears once; the two slots 2r and 2r + 1 hold blocks whose numbers sum to 15. `doc_lengths`: the lengths sum to 8192 and the longest is exactly 2048.
All inputs are finite; a program needn't handle non-finite values.
Results may differ from a plain program's by a relative error of at most 0.019.
Values may be sent and summed in bfloat16 or wider, within the bound.
No kernel may reach another device: no remote copies, remote signals or barrier semaphores. Data moves between devices by JAX's collectives and lax.ppermute only.
A program may use at most 128 MiB of HBM per device.

v0:
```python
import math

import jax
import jax.numpy as jnp
from jax import lax
from jax.sharding import PartitionSpec as P

HD = 128
GROUP = 4


neg_large = -1e30


def slot_lookup(slots, span_slots):
    table = jnp.arange(span_slots.shape[0], dtype=jnp.int32)
    hits = slots[:, None] == table[None, :]
    return jnp.sum(jnp.where(hits, span_slots[None, :], 0), axis=1)


def doc_lookup(positions, doc_ends):
    return jnp.sum((positions[:, None] >= doc_ends[None, :]).astype(jnp.int32), axis=1)


def shards(tokens, norm_gain, w_qkv, w_out, doc_lengths, span_slots):
    n_tp = lax.axis_size("tp")
    ctx_rank = lax.axis_index("ctx")
    local_rows = tokens.shape[0] * n_tp
    span = local_rows // 2
    groups = w_qkv.shape[1] // ((GROUP + 2) * HD)
    scale = 1.0 / HD**0.5
    doc_ends = jnp.cumsum(doc_lengths)
    values_in = tokens.astype(jnp.float32)
    mean_sq = jnp.mean(values_in * values_in, axis=-1, keepdims=True)
    normed = (values_in * lax.rsqrt(mean_sq + 1e-05) * norm_gain).astype(jnp.bfloat16)
    own_slots = lax.dynamic_slice_in_dim(span_slots, 2 * ctx_rank, 2, 0)
    offsets = jnp.arange(span, dtype=jnp.int32)
    query_pos = [own_slots[half] * span + offsets for half in range(2)]
    query_doc = [doc_lookup(query_pos[half], doc_ends) for half in range(2)]

    def start_state():
        state_max = jnp.full((groups, GROUP, span), neg_large, jnp.float32)
        state_sum = jnp.zeros((groups, GROUP, span), jnp.float32)
        state_acc = jnp.zeros((groups, GROUP, span, HD), jnp.float32)
        return (state_max, state_sum, state_acc)

    qkv = jnp.dot(
        lax.all_gather(normed, "tp", axis=0, tiled=True), w_qkv, preferred_element_type=jnp.float32
    ).astype(jnp.bfloat16)
    qkv = qkv.reshape(local_rows, groups, GROUP + 2, HD)
    queries = qkv[:, :, :GROUP, :]
    keys = qkv[:, :, GROUP, :].reshape(local_rows, groups * HD)
    values = qkv[:, :, GROUP + 1, :].reshape(local_rows, groups * HD)
    key_rows = lax.all_gather(keys, "ctx", axis=0, tiled=True)
    q_halves = jnp.transpose(queries.reshape(2, span, groups, GROUP, HD), (0, 2, 3, 1, 4))
    count = key_rows.shape[0]
    key_block = math.gcd(count, 512)
    n_blocks = count // key_block
    index = jnp.arange(count, dtype=jnp.int32)
    key_pos = slot_lookup(index // span, span_slots) * span + index % span
    key_doc = doc_lookup(key_pos, doc_ends)
    keys_b = key_rows.reshape(n_blocks, key_block, groups, HD)
    values_b = lax.all_gather(values, "ctx", axis=0, tiled=True).reshape(
        n_blocks, key_block, groups, HD
    )
    pos_b = key_pos.reshape(n_blocks, key_block)
    doc_b = key_doc.reshape(n_blocks, key_block)

    def step(states, block):
        kblk, vblk, kpos, kdoc = block
        updated = []
        for half in range(2):
            qpos = query_pos[half]
            qdoc = query_doc[half]
            needed = (
                (jnp.min(kpos) <= jnp.max(qpos))
                & (jnp.max(kdoc) >= jnp.min(qdoc))
                & (jnp.min(kdoc) <= jnp.max(qdoc))
            )

            def update(state, qpos=qpos, qdoc=qdoc, half=half):
                state_max, state_sum, state_acc = state
                scores = (
                    jnp.einsum(
                        "gqcd,kgd->gqck", q_halves[half], kblk, preferred_element_type=jnp.float32
                    )
                    * scale
                )
                allowed = (kpos[None, :] <= qpos[:, None]) & (kdoc[None, :] == qdoc[:, None])
                masked = jnp.where(allowed[None, None], scores, jnp.float32(neg_large))
                new_max = jnp.maximum(state_max, jnp.max(masked, axis=-1))
                expo = jnp.where(
                    allowed[None, None], jnp.exp(masked - new_max[..., None]), jnp.float32(0.0)
                )
                factor = jnp.exp(state_max - new_max)
                new_sum = state_sum * factor + jnp.sum(expo, axis=-1)
                product = jnp.einsum(
                    "gqck,kgd->gqcd",
                    expo.astype(jnp.bfloat16),
                    vblk,
                    preferred_element_type=jnp.float32,
                )
                new_acc = state_acc * factor[..., None] + product
                return (new_max, new_sum, new_acc)

            updated.append(lax.cond(needed, update, lambda state: state, states[half]))
        return ((updated[0], updated[1]), None)

    final, unused = lax.scan(step, (start_state(), start_state()), (keys_b, values_b, pos_b, doc_b))
    outputs = []
    for half in range(2):
        state_max, state_sum, state_acc = final[half]
        outputs.append((state_acc / state_sum[..., None]).astype(jnp.bfloat16))
    stacked = jnp.stack(outputs, axis=0)
    heads = jnp.transpose(stacked, (0, 3, 1, 2, 4)).reshape(local_rows, groups * GROUP * HD)
    return lax.psum_scatter(
        jnp.dot(heads, w_out, preferred_element_type=jnp.float32).astype(jnp.bfloat16),
        "tp",
        scatter_dimension=0,
        tiled=True,
    )


def solution(mesh):
    placed = (P(("dp", "ctx", "tp"), None), P(), P(None, "tp"), P("tp", None), P("dp"), P("dp"))
    return jax.shard_map(
        shards, mesh=mesh, in_specs=placed, out_specs=P(("dp", "ctx", "tp"), None), check_vma=False
    )
```

profile of v0, /device:TPU:18, one launch (start us, length us, event | category | flops | bytes accessed | tf_op | source)
XLA Modules:
  0.0 524.1 jit_solution(12504136971439899261)
XLA Ops:
  6.5 2.1 fusion.46
  8.6 3.5 fusion.48
  12.2 87.4 %all-gather.6.cloned.1.call-done = bf16[1024,8192]{1,0:T(8,128)(2,1)} async-done(((bf16[128,8192]{1,0:T(8,128)(2,1)}), bf16[1024,8192]{1,0:T(8,128)(2,1)}) %all-gather.6.cloned.1.call-update) | async-done | bytes 16777232 | tf_op jit(solution)/shard_map/all_gather | solution.py:48
  99.7 18.3 %convolution_convert_fusion.1 = bf16[1024,768]{0,1:T(8,128)(2,1)S(1)} fusion(bf16[1024,8192]{1,0:T(8,128)(2,1)} %all-gather.6.cloned.1.call-done, bf16[8192,768]{1,0:T(8,128)(2,1)} %param.14), kind=kOutput, calls=%fused_computation.58 | convolution fusion | flops 12885688320 | bytes 30932992 | tf_op jit(solution)/shard_map/dot_general | solution.py:47
  123.9 1.3 slice.28
  126.2 43.4 %all-gather.8.cloned.1.call-done = bf16[8192,1,1,128]{0,3,2,1:T(8,128)(2,1)} async-done(((bf16[1024,1,1,128]{0,3,2,1:T(8,128)(2,1)}), bf16[8192,1,1,128]{0,3,2,1:T(8,128)(2,1)}) %all-gather.8.cloned.1.call-update) | async-done | bytes 2097168 | tf_op jit(solution)/shard_map/all_gather | solution.py:54
  169.6 4.1 copy.23
  173.7 49.0 %all-gather.10.cloned.1.call-done = bf16[8192,1,1,128]{0,3,2,1:T(8,128)(2,1)} async-done(((bf16[1024,1,1,128]{0,3,2,1:T(8,128)(2,1)}), bf16[8192,1,1,128]{0,3,2,1:T(8,128)(2,1)}) %all-gather.10.cloned.1.call-update) | async-done | bytes 2097168 | tf_op jit(solution)/shard_map/all_gather | solution.py:63
  222.7 4.1 copy.24
  227.0 162.7 %while.22 = (s32[]{:T(128)}, f32[1,4,512]{2,1,0:T(4,128)S(1)}, f32[1,4,512]{2,1,0:T(4,128)S(1)}, f32[1,4,512,128]{3,2,1,0:T(8,128)S(1)}, f32[1,4,512]{2,1,0:T(4,...) while((s32[]{:T(128)}, f32[1,4,512]{2,1,0:T(4,128)S(1)}, ...), condition=%wide.region_24.25_spmd.clone, body=%wide.region_12.24_spmd.clone.sunk | while | flops 1103641088 | bytes 33854036 | solution.py:109
  227.7 1.0 dynamic-slice_bitcast_fusion.3
  236.8 1.0 dynamic-slice_bitcast_fusion.3
  246.0 1.0 dynamic-slice_bitcast_fusion.3
  255.2 1.0 dynamic-slice_bitcast_fusion.3
  264.4 1.0 dynamic-slice_bitcast_fusion.3
  272.9 3.9 conditional.6
  274.1 1.0 fusion.6
  275.2 1.7 fusion.13
  277.5 1.0 dynamic-slice_bitcast_fusion.3
  282.2 3.9 conditional.7
  283.4 1.0 fusion.27
  284.5 1.7 fusion.34
  290.7 1.0 dynamic-slice_bitcast_fusion.3
  309.0 1.0 dynamic-slice_bitcast_fusion.3
  326.7 3.9 conditional.6
  327.9 1.0 fusion.6
  329.0 1.7 fusion.13
  372.7 3.9 conditional.7
  374.0 1.0 fusion.27
  375.0 1.7 fusion.34
  391.3 15.1 %convolution_convert_fusion = bf16[1024,8192]{1,0:T(8,128)(2,1)} fusion(bf16[512,8192]{1,0:T(8,128)(2,1)} %param.15, bf16[128,8,4,128]{3,2,1,0:T(4,128)(2,1)S(1)} %bitcast.101), kind=kOutput, calls=%fused_computation.52 | convolution fusion | flops 8598323200 | bytes 26214400 | tf_op jit(solution)/shard_map/dot_general | solution.py:117
  406.5 111.1 %reduce-scatter.2.cloned.1.call-done = bf16[128,8192]{1,0:T(8,128)(2,1)} async-done(((bf16[1024,8192]{1,0:T(8,128)(2,1)}), bf16[128,8192]{1,0:T(8,128)(2,1)}) %reduce-scatter.2.cloned.1.call-update) | async-done | bytes 2097168 | tf_op jit(solution)/shard_map/reduce_scatter | solution.py:116
  (153 shorter events, 31.4 us)
Async XLA Ops:
  6.5 93.1 %all-gather.6.cloned.1.call-start = ((), (), s32[]{:S(2)}) async-start(), calls=%async_computation.1 | async-start | bytes 18874368 | tf_op jit(solution)/shard_map/all_gather | solution.py:48
  12.1 107.5 %copy-start.1 = (s32[16]{0:T(128)S(1)}, s32[16]{0:T(128)}, u32[]{:S(2)}) copy-start(s32[16]{0:T(128)} %param.17) | copy-start | bytes 196
  12.2 109.6 %copy-start.2 = (s32[16]{0:T(128)S(1)}, s32[16]{0:T(128)}, u32[]{:S(2)}) copy-start(s32[16]{0:T(128)} %param.16) | copy-start | bytes 196
  12.2 157.4 %all-gather.8.cloned.1.call-start = ((), (), s32[]{:S(2)}) async-start(), calls=%async_computation.3 | async-start | bytes 2359296 | tf_op jit(solution)/shard_map/all_gather | solution.py:54
  117.9 6.0 %copy-start = (bf16[1024,768]{0,1:T(8,128)(2,1)}, bf16[1024,768]{0,1:T(8,128)(2,1)S(1)}, u32[]{:S(2)}) copy-start(bf16[1024,768]{0,1:T(8,128)(2,1)S(1)} %convolution_convert_fusion.1) | copy-start | bytes 4718596
  118.9 103.8 %all-gather.10.cloned.1.call-start = ((), (), s32[]{:S(2)}) async-start(), calls=%async_computation.4 | async-start | bytes 2359296 | tf_op jit(solution)/shard_map/all_gather | solution.py:63
  119.6 398.0 %reduce-scatter.2.cloned.1.call-start = ((), (), s32[]{:S(2)}) async-start(), calls=%async_computation.2 | async-start | bytes 18874368 | tf_op jit(solution)/shard_map/reduce_scatter | solution.py:116
Sparse Core Ops, SparseCore 0:
  12.3 87.3 all-gather.5
  119.0 50.5 all-gather.7
  171.3 51.3 all-gather.9
  406.6 110.9 reduce-scatter.1
where the time goes:
time: 527 us; the launch traced here: 524 us
  waiting for transfers between devices  292 us (55%)
  loops' own time  120 us (23%)
  matrix products  43.5 us (8%)
  local copies, waits for them, and re-layouts  29 us (6%)
  other arithmetic  24.8 us (5%)
  between operations  14.6 us (3%)
    another operation x1, loops' own time, shards(): lax.scan(step, (start_state(), start_state()), (keys_b, values_b, pos_b,...  120 us
    reduce_scatter x1, waiting for transfers between devices, shards(): lax.psum_scatter(jnp.dot(heads, w_out, preferred_element_type=jnp.float32...  111 us
    all_gather x1, waiting for transfers between devices, shards(): lax.all_gather(normed, 'tp', axis=0, tiled=True)  87.4 us
    all_gather x1, waiting for transfers between devices, shards(): lax.all_gather(values, 'ctx', axis=0, tiled=True)  49 us
    all_gather x1, waiting for transfers between devices, shards(): key_rows = lax.all_gather(keys, 'ctx', axis=0, tiled=True)  43.4 us
    dot_general x1, matrix products, shards(): jnp.dot(lax.all_gather(normed, 'tp', axis=0, tiled=True), w_qkv, preferre...  18.3 us
    squeeze x16, local copies, waits for them, and re-layouts, shards(): lax.scan(step, (start_state(), start_state()), (keys_b, values_b, pos_b,...  15.8 us
    dot_general x1, matrix products, shards(): jnp.dot(heads, w_out, preferred_element_type=jnp.float32)  15.1 us
  transfers between devices with their start and end apart: 4, of which 4 were waited for; matrix products, arithmetic and copies ran while one was open for 2% of the time, Pallas kernels for 0%

commit v1 on v0

v1 whole, which is shorter than its diff:
```python
import functools

import jax
import jax.numpy as jnp
from jax import lax
from jax.experimental import pallas as pl
from jax.experimental.pallas import tpu as pltpu
from jax.sharding import PartitionSpec as P

HD = 128
GROUP = 4
QW = GROUP * HD
NZ = 4
NX = 4
TILE = 128
KTILE = 256
MIB = 1 << 20
MASKED = -3e38
LOWEST = -2e31
LOG2E = 1.4426950408889634

Z_BASE = (0, 512, 768, 256)


def z_perm(dz, dc):
    return [
        (z * 2 + c, ((z + dz) % NZ) * 2 + (c + dc) % 2) for z in range(NZ) for c in range(2)
    ]


def x_perm(dx, dy):
    return [
        (x * 2 + y, ((x + dx) % NX) * 2 + (y + dy) % 2) for x in range(NX) for y in range(2)
    ]


def z_send(value, dz):
    return lax.ppermute(value, "tp", z_perm(dz, 0))


def swap(value):
    return lax.ppermute(value, "tp", z_perm(0, 1))


def x_send(value, dx):
    return lax.ppermute(value, "ctx", x_perm(dx, 0))


def y_swap(value):
    return lax.ppermute(value, "ctx", x_perm(0, 1))


def cost(flops, nbytes, trans=0):
    return pl.CostEstimate(flops=int(flops), bytes_accessed=int(nbytes), transcendentals=int(trans))


def norm_body(x_ref, gain_ref, out_ref):
    x = x_ref[...].astype(jnp.float32)
    mean_sq = jnp.mean(x * x, axis=-1, keepdims=True)
    out_ref[...] = (x * lax.rsqrt(mean_sq + 1e-05) * gain_ref[...]).astype(jnp.bfloat16)


def norm_piece(tokens, gain, piece, rows):
    width = tokens.shape[1]
    block = rows // 2
    return pl.pallas_call(
        norm_body,
        grid=(2,),
        in_specs=[
            pl.BlockSpec((block, width), lambda i: (piece * 2 + i, 0)),
            pl.BlockSpec((1, width), lambda i: (0, 0)),
        ],
        out_specs=pl.BlockSpec((block, width), lambda i: (i, 0)),
        out_shape=jax.ShapeDtypeStruct((rows, width), jnp.bfloat16),
        cost_estimate=cost(6 * rows * width, 4 * rows * width),
        compiler_params=pltpu.CompilerParams(vmem_limit_bytes=16 * MIB),
        name="norm_piece",
    )(tokens, gain)


def project_body(n_in, widths, *refs):
    xs, w_ref = refs[:n_in], refs[n_in]
    outs, acc = refs[n_in + 1 : -1], refs[-1]
    step = pl.program_id(0)
    rows = jnp.concatenate([x[...] for x in xs], axis=0)
    part = jnp.dot(rows, w_ref[...], preferred_element_type=jnp.float32)

    @pl.when(step == 0)
    def _():
        acc[...] = part

    @pl.when(step > 0)
    def _():
        acc[...] += part

    @pl.when(step == pl.num_programs(0) - 1)
    def _():
        at = 0
        for out, width in zip(outs, widths):
            out[...] = acc[:, at : at + width].astype(jnp.bfloat16)
            at += width


def project(xs, w, first, widths, depth=1024):
    total = sum(widths)
    rows = sum(x.shape[0] for x in xs)
    width = w.shape[0]
    column = first // total
    return pl.pallas_call(
        functools.partial(project_body, len(xs), widths),
        grid=(width // depth,),
        in_specs=[pl.BlockSpec((x.shape[0], depth), lambda k: (0, k)) for x in xs]
        + [pl.BlockSpec((depth, total), lambda k: (k, column))],
        out_specs=[pl.BlockSpec((rows, one), lambda k: (0, 0)) for one in widths],
        out_shape=[jax.ShapeDtypeStruct((rows, one), jnp.bfloat16) for one in widths],
        scratch_shapes=[pltpu.VMEM((rows, total), jnp.float32)],
        cost_estimate=cost(2 * rows * width * total, 2 * width * (rows + total)),
        compiler_params=pltpu.CompilerParams(vmem_limit_bytes=24 * MIB),
        name="project",
    )(*xs, w)


def exchange(kv):
    other = y_swap(kv)
    left0, left1 = x_send(kv, 1), x_send(other, 1)
    right0, right1 = x_send(kv, -1), x_send(other, -1)
    far0, far1 = x_send(left0, 1), x_send(right1, -1)
    return [kv, other, right0, right1, far0, far1, left0, left1]


def attend_body(n_doc, n_kv, offsets, table_ref, ends_ref, starts_ref, q_ref, *refs):
    kv_hbm = refs[:n_kv]
    keep_ref, send_ref, kv, sem = refs[n_kv:]
    tile = pl.program_id(0)

    def copies():
        return [
            pltpu.make_async_copy(src, kv.at[pl.ds(at, src.shape[0])], sem.at[i])
            for i, (src, at) in enumerate(zip(kv_hbm, offsets))
        ]

    @pl.when(tile == 0)
    def _():
        for one in copies():
            one.start()
        for one in copies():
            one.wait()

    start = starts_ref[tile]
    q = jnp.concatenate([q_ref[:, h * HD : (h + 1) * HD] for h in range(GROUP)], axis=0)
    rows = GROUP * TILE
    q_pos = start + lax.rem(lax.broadcasted_iota(jnp.int32, (rows, 1), 0), TILE)
    doc_start = jnp.zeros((rows, 1), jnp.int32)
    first = jnp.int32(0)
    for i in range(n_doc):
        end = ends_ref[i]
        doc_start = jnp.where(q_pos >= end, end, doc_start)
        first = jnp.where(start >= end, end, first)
    scale = LOG2E / HD**0.5
    ratio = KTILE // TILE

    def step(at, state):
        top, total, acc = state
        spots = [pl.multiple_of(table_ref[at * ratio + i], TILE) for i in range(ratio)]
        keys = jnp.concatenate([kv[pl.ds(spot, TILE), :HD] for spot in spots], axis=0)
        vals = jnp.concatenate([kv[pl.ds(spot, TILE), HD:] for spot in spots], axis=0)
        s = lax.dot_general(q, keys, (((1,), (1,)), ((), ())), preferred_element_type=jnp.float32)
        k_pos = at * KTILE + lax.broadcasted_iota(jnp.int32, (rows, KTILE), 1)
        allowed = (k_pos <= q_pos) & (k_pos >= doc_start)
        s = jnp.where(allowed, s, MASKED)
        new_top = jnp.maximum(top, jnp.max(s, axis=-1, keepdims=True))
        e = jnp.exp2((s - new_top) * scale)
        factor = jnp.exp2((top - new_top) * scale)
        total = total * factor + jnp.sum(e, axis=-1, keepdims=True)
        acc = acc * factor + jnp.dot(
            e.astype(jnp.bfloat16), vals, preferred_element_type=jnp.float32
        )
        return new_top, total, acc

    state = (
        jnp.full((rows, 1), LOWEST, jnp.float32),
        jnp.zeros((rows, 1), jnp.float32),
        jnp.zeros((rows, HD), jnp.float32),
    )
    top, total, acc = lax.fori_loop(first // KTILE, (start + TILE - 1) // KTILE + 1, step, state)
    out = (acc / total).astype(jnp.bfloat16)
    out = jnp.concatenate([out[h * TILE : (h + 1) * TILE] for h in range(GROUP)], axis=1)

    @pl.when(lax.rem(tile, 2) == 0)
    def _():
        keep_ref[...] = out

    @pl.when(lax.rem(tile, 2) == 1)
    def _():
        send_ref[...] = out


def attend(q, kvs, offsets, table, ends, starts, span):
    tiles = q.shape[0] // TILE
    half = q.shape[0] // 2
    count = sum(kv.shape[0] for kv in kvs)
    any_spec = pl.BlockSpec(memory_space=pl.ANY)
    spec = pltpu.PrefetchScalarGridSpec(
        num_scalar_prefetch=3,
        grid=(tiles,),
        in_specs=[pl.BlockSpec((TILE, QW), lambda i, *_: (i, 0))] + [any_spec] * len(kvs),
        out_specs=[pl.BlockSpec((TILE, QW), lambda i, *_: (i // 2, 0))] * 2,
        scratch_shapes=[
            pltpu.VMEM((count, 2 * HD), jnp.bfloat16),
            pltpu.SemaphoreType.DMA((len(kvs),)),
        ],
    )
    return pl.pallas_call(
        functools.partial(attend_body, ends.shape[0], len(kvs), offsets),
        grid_spec=spec,
        out_shape=[jax.ShapeDtypeStruct((half, QW), jnp.bfloat16)] * 2,
        cost_estimate=cost(
            tiles * 4 * GROUP * TILE * span * HD * 2,
            count * 4 * HD + q.size * 4,
            tiles * GROUP * TILE * span,
        ),
        compiler_params=pltpu.CompilerParams(vmem_limit_bytes=32 * MIB),
        name="attend",
    )(table, ends, starts, q, *kvs)


def out_body(own_ref, sib_ref, w_own, w_sib, *outs):
    sums = jnp.dot(own_ref[...], w_own[...], preferred_element_type=jnp.float32)
    sums += jnp.dot(sib_ref[...], w_sib[...], preferred_element_type=jnp.float32)
    for i, out in enumerate(outs):
        out[...] = sums[i * TILE : (i + 1) * TILE].astype(jnp.bfloat16)


def out_project(own, sib, w_own, w_sib, half, step=1024):
    depth, width = w_own.shape
    part = width // 2
    rows = own.shape[0]
    n_out = rows // TILE
    first = half * part // step
    return pl.pallas_call(
        out_body,
        grid=(part // step,),
        in_specs=[pl.BlockSpec((rows, depth), lambda n: (0, 0))] * 2
        + [pl.BlockSpec((depth, step), lambda n: (0, first + n))] * 2,
        out_specs=[pl.BlockSpec((TILE, step), lambda n: (0, n))] * n_out,
        out_shape=[jax.ShapeDtypeStruct((TILE, part), jnp.bfloat16)] * n_out,
        cost_estimate=cost(
            4 * rows * depth * part, 4 * depth * part + 4 * rows * depth + 2 * rows * part
        ),
        compiler_params=pltpu.CompilerParams(vmem_limit_bytes=24 * MIB),
        name="out_project",
    )(own, sib, w_own, w_sib)


def final_body(p_lo, p_hi, a_lo, a_hi, b_lo, b_hi, out_ref):
    f32 = jnp.float32
    half = p_lo.shape[1]
    lo = p_lo[...].astype(f32) + a_lo[...].astype(f32) + b_lo[...].astype(f32)
    hi = p_hi[...].astype(f32) + a_hi[...].astype(f32) + b_hi[...].astype(f32)
    out_ref[:, :half] = lo.astype(jnp.bfloat16)
    out_ref[:, half:] = hi.astype(jnp.bfloat16)


def final_sum(*parts):
    rows, half = parts[0].shape
    block = 32
    return pl.pallas_call(
        final_body,
        grid=(rows // block,),
        in_specs=[pl.BlockSpec((block, half), lambda i: (i, 0))] * 6,
        out_specs=pl.BlockSpec((block, 2 * half), lambda i: (i, 0)),
        out_shape=jax.ShapeDtypeStruct((rows, 2 * half), jnp.bfloat16),
        cost_estimate=cost(6 * rows * half, 16 * rows * half),
        compiler_params=pltpu.CompilerParams(vmem_limit_bytes=24 * MIB),
        name="final_sum",
    )(*parts)


def add_parts(a, b):
    return (a.astype(jnp.float32) + b.astype(jnp.float32)).astype(jnp.bfloat16)


def shards(tokens, norm_gain, w_qkv, w_out, doc_lengths, span_slots):
    ctx = lax.axis_index("ctx")
    tp = lax.axis_index("tp")
    x, y, z, core = ctx // 2, ctx % 2, tp // 2, tp % 2
    piece = tokens.shape[0] // 2
    gain = norm_gain.reshape(1, -1)

    n_spans = span_slots.shape[0]
    per_span = 4
    span = per_span * TILE
    ends = jnp.cumsum(doc_lengths).astype(jnp.int32)
    numbers = jnp.arange(n_spans, dtype=jnp.int32)
    slot_of = jnp.sum(
        jnp.where(span_slots[None, :] == numbers[:, None], numbers[None, :], 0), axis=1
    )
    tile_no = jnp.arange(per_span, dtype=jnp.int32)[None, :]
    slot = slot_of[:, None]
    tile_tp = (slot % 2) * per_span + tile_no
    rank = slot // 2
    rel_z = (tile_tp // 2 - z) % NZ
    z_base = jnp.where(rel_z == 0, Z_BASE[0], 0)
    for i in range(1, NZ):
        z_base = jnp.where(rel_z == i, Z_BASE[i], z_base)
    rel_src = ((rank // 2 - x) % NX) * 2 + (rank % 2 != y).astype(jnp.int32)
    table = rel_src * 1024 + z_base + (tile_tp % 2 != core).astype(jnp.int32) * TILE
    table = table.reshape(-1).astype(jnp.int32)
    own_spans = lax.dynamic_slice_in_dim(span_slots, 2 * ctx, 2, 0)

    def starts_of(*dzs):
        tps = jnp.stack([((z + dz) % NZ) * 2 + c for dz in dzs for c in (core, 1 - core)])
        blocks = jnp.where(tps // per_span == 0, own_spans[0], own_spans[1])
        return (blocks * span + (tps % per_span) * TILE).astype(jnp.int32)

    n0 = norm_piece(tokens, gain, 0, piece)
    n1 = norm_piece(tokens, gain, 1, piece)
    lo0, hi0 = z_send(n0, 1), z_send(n0, -1)
    lo1, hi1 = z_send(n1, 1), z_send(n1, -1)
    far0, far1 = z_send(lo0, 1), z_send(hi1, -1)
    group_a = [n0, n1, swap(n0), swap(n1)]
    group_b = [lo0, lo1, swap(lo0), swap(lo1), hi0, hi1, swap(hi0), swap(hi1)]
    group_d = [far0, far1, swap(far0), swap(far1)]
    w_sib = swap(w_out)

    q_a, kv_a = project(group_a, w_qkv, 0, (QW, 2 * HD))
    q_b, kv_b = project(group_b, w_qkv, 0, (QW, 2 * HD))
    (kv_d,) = project(group_d, w_qkv, QW, (2 * HD,))
    (q_d,) = project(group_d, w_qkv, 0, (QW,))
    kvs, offsets = [], []
    for kv, base in ((kv_a, 0), (kv_b, 256), (kv_d, 768)):
        for i, one in enumerate(exchange(kv)):
            kvs.append(one)
            offsets.append(i * 1024 + base)

    def heads_of(q, *dzs):
        keep, send = attend(q, kvs, offsets, table, ends, starts_of(*dzs), 1024)
        return keep, swap(send)

    d_own, d_sib = heads_of(q_d, 2)
    (d_lo,) = out_project(d_own, d_sib, w_out, w_sib, 0)
    (d_hi,) = out_project(d_own, d_sib, w_out, w_sib, 1)
    from_low, from_high = z_send(d_lo, 1), z_send(d_hi, -1)
    b_own, b_sib = heads_of(q_b, -1, 1)
    prev_lo, next_lo = out_project(b_own, b_sib, w_out, w_sib, 0)
    prev_hi, next_hi = out_project(b_own, b_sib, w_out, w_sib, 1)
    early_hi, early_lo = z_send(next_hi, 1), z_send(prev_lo, -1)
    late_lo = z_send(add_parts(next_lo, from_low), 1)
    late_hi = z_send(add_parts(prev_hi, from_high), -1)
    a_own, a_sib = heads_of(q_a, 0)
    (a_lo,) = out_project(a_own, a_sib, w_out, w_sib, 0)
    (a_hi,) = out_project(a_own, a_sib, w_out, w_sib, 1)
    return final_sum(a_lo, a_hi, early_lo, early_hi, late_lo, late_hi)


def solution(mesh):
    placed = (P(("dp", "ctx", "tp"), None), P(), P(None, "tp"), P("tp", None), P("dp"), P("dp"))
    return jax.shard_map(
        shards, mesh=mesh, in_specs=placed, out_specs=P(("dp", "ctx", "tp"), None), check_vma=False
    )
```

time: 527 us -> 297 us (0.56)
  waiting for transfers between devices: 292 us -> 107 us
  loops' own time: 120 us -> 0 us
  Pallas kernels: 0 us -> 101 us
  starting transfers between devices: 0.12 us -> 50.1 us
  matrix products: 43.5 us -> 0 us
  other arithmetic: 24.8 us -> 5.38 us
  between operations: 14.6 us -> 0.95 us
    all_gather x3 -> x0, waiting for transfers between devices: 180 us -> none  [the longest x1 87.4 us: shards(): lax.all_gather(normed, 'tp', axis=0, tiled=True)]
    another operation x33 -> x0, loops' own time: 120 us -> none  [the longest x1 120 us: shards(): lax.scan(step, (start_state(), start_state()), (keys_b, values_b, pos_b,...]
    reduce_scatter x1 -> x0, waiting for transfers between devices: 111 us -> none  [shards(): lax.psum_scatter(jnp.dot(heads, w_out, preferred_element_type=jnp.float32...]
    ppermute x0 -> x45, waiting for transfers between devices: none -> 107 us  [the longest x12 89.1 us: z_send(): return lax.ppermute(value, 'tp', z_perm(dz, 0))]
    pallas_call x0 -> x16, Pallas kernels: none -> 101 us  [the longest x3 43 us: attend(): pl.pallas_call(functools.partial(attend_body, ends.shape[0], len(kvs), of...]
    ppermute x0 -> x45, starting transfers between devices: none -> 50.1 us  [the longest x18 23.1 us: x_send(): return lax.ppermute(value, 'ctx', x_perm(dx, 0))]
    dot_general x10 -> x0, matrix products: 43.5 us -> none  [the longest x1 18.3 us: shards(): jnp.dot(lax.all_gather(normed, 'tp', axis=0, tiled=True), w_qkv, preferre...]
    unnamed x8 -> x114, local copies, waits for them, and re-layouts: 0.93 us -> 30.3 us
  transfers between devices with their start and end apart: 4 -> 45, of which waited for: 4 -> 14; matrix products, arithmetic and copies ran while one was open for 2% -> 3% of each run, Pallas kernels for 0% -> 32%
where the time goes in v1:
time: 297 us
  waiting for transfers between devices  107 us (36%)
  Pallas kernels  101 us (34%)
  starting transfers between devices  50.1 us (17%)
  local copies, waits for them, and re-layouts  32.5 us (11%)
  other arithmetic  5.38 us (2%)
    ppermute x12, waiting for transfers between devices, z_send(): return lax.ppermute(value, 'tp', z_perm(dz, 0))  89.1 us
    pallas_call x3, Pallas kernels, attend(): pl.pallas_call(functools.partial(attend_body, ends.shape[0], len(kvs), of...  43 us
    unnamed x114, local copies, waits for them, and re-layouts  30.3 us
    pallas_call x4, Pallas kernels, project(): pl.pallas_call(functools.partial(project_body, len(xs), widths), grid=(wi...  27.5 us
    pallas_call x6, Pallas kernels, out_project(): pl.pallas_call(out_body, grid=(part // step,), in_specs=[pl.BlockSpec((ro...  27.1 us
    ppermute x18, starting transfers between devices, x_send(): return lax.ppermute(value, 'ctx', x_perm(dx, 0))  23.1 us
    ppermute x12, starting transfers between devices, z_send(): return lax.ppermute(value, 'tp', z_perm(dz, 0))  21.6 us
    ppermute x18, waiting for transfers between devices, x_send(): return lax.ppermute(value, 'ctx', x_perm(dx, 0))  12.2 us
  transfers between devices with their start and end apart: 45, of which 14 were waited for; matrix products, arithmetic and copies ran while one was open for 3% of the time, Pallas kernels for 32%

profile of v1, /device:TPU:18, one launch (start us, length us, event | category | flops | bytes accessed | tf_op | source)
XLA Modules:
  0.0 296.8 jit_solution(13542842540089416501)
XLA Ops:
  3.0 4.1 %collective-permute-start.13 = (bf16[64,8192]{1,0:T(8,128)(2,1)S(1)}, bf16[64,8192]{1,0:T(8,128)(2,1)S(1)}, u32[]{:S(2)}, u32[]{:S(2)}) collective-permute-start(bf16[64,8192]{1,0:T(8,128)(2,1)S(1)} %norm_piece.2.refs_0_), channel_id=1, source_target_pairs={{0,12},{2,14},{4,0},{6,2},{8,4},{10,6},{12,8},{14,10},{1,13},{3,15... | collective-permute-start | bytes 3145736 | tf_op jit(solution)/shard_map/ppermute | solution.py:38
  8.4 21.8 %collective-permute-done.13.refs_4_ = bf16[64,8192]{1,0:T(8,128)(2,1)S(1)} collective-permute-done((bf16[64,8192]{1,0:T(8,128)(2,1)S(1)}, bf16[64,8192]{1,0:T(8,128)(2,1)S(1)}, u32[]{:S(2)}, u32[]{:S(2)}) %collective-permute-start.13) | collective-permute-done | bytes 1048608 | tf_op jit(solution)/shard_map/ppermute | solution.py:38
  30.2 3.7 %collective-permute-start.14 = (bf16[64,8192]{1,0:T(8,128)(2,1)S(1)}, bf16[64,8192]{1,0:T(8,128)(2,1)S(1)}, u32[]{:S(2)}, u32[]{:S(2)}) collective-permute-start(bf16[64,8192]{1,0:T(8,128)(2,1)S(1)} %norm_piece.3.refs_1_), channel_id=1, source_target_pairs={{0,12},{2,14},{4,0},{6,2},{8,4},{10,6},{12,8},{14,10},{1,13},{3,15... | collective-permute-start | bytes 3145736 | tf_op jit(solution)/shard_map/ppermute | solution.py:38
  34.1 4.6 %copy-done.2 = bf16[8192,768]{1,0:T(8,128)(2,1)S(1)} copy-done((bf16[8192,768]{1,0:T(8,128)(2,1)S(1)}, bf16[8192,768]{1,0:T(8,128)(2,1)}, u32[]{:S(2)}) %copy-start.2) | copy-done | bytes 12582936
  38.7 5.6 %project.4 = (bf16[256,512]{1,0:T(8,128)(2,1)S(1)}, bf16[256,256]{1,0:T(8,128)(2,1)S(1)}) custom-call(bf16[64,8192]{1,0:T(8,128)(2,1)S(1)} %norm_piece.2.refs_0_, bf16[64,8192]{1,0:T(8,128)(2,1)S(1)} %norm_piece.3.refs_1_, bf16[64,8192]{1,0:T(8,128)(2,1)S(1)} %collective-permute-done.refs_2_, bf16[64,8192]{1,0:T(8,128)(2,1)S(1)} %collective-permute-done.1.refs_3_, ...), custom_call_target="tpu_custom_call" | custom-call | flops 3221225472 | bytes 16777216 | tf_op jit(solution)/shard_map/project/pallas_call | solution.py:109
  45.0 11.2 %collective-permute-done.14.refs_5_ = bf16[64,8192]{1,0:T(8,128)(2,1)S(1)} collective-permute-done((bf16[64,8192]{1,0:T(8,128)(2,1)S(1)}, bf16[64,8192]{1,0:T(8,128)(2,1)S(1)}, u32[]{:S(2)}, u32[]{:S(2)}) %collective-permute-start.14) | collective-permute-done | bytes 1048608 | tf_op jit(solution)/shard_map/ppermute | solution.py:38
  57.7 3.5 %collective-permute-done.10.refs_1_ = bf16[64,8192]{1,0:T(8,128)(2,1)S(1)} collective-permute-done((bf16[64,8192]{1,0:T(8,128)(2,1)S(1)}, bf16[64,8192]{1,0:T(8,128)(2,1)S(1)}, u32[]{:S(2)}, u32[]{:S(2)}) %collective-permute-start.10) | collective-permute-done | bytes 1048608 | tf_op jit(solution)/shard_map/ppermute | solution.py:38
  67.7 3.5 %collective-permute-done.6.refs_4_ = bf16[256,256]{1,0:T(8,128)(2,1)S(1)} collective-permute-done((bf16[256,256]{1,0:T(8,128)(2,1)S(1)}, bf16[256,256]{1,0:T(8,128)(2,1)S(1)}, u32[]{:S(2)}, u32[]{:S(2)}) %collective-permute-start.6) | collective-permute-done | bytes 131104 | tf_op jit(solution)/shard_map/ppermute | solution.py:46
  71.4 10.7 %collective-permute-done.24.refs_0_ = bf16[64,8192]{1,0:T(8,128)(2,1)S(1)} collective-permute-done((bf16[64,8192]{1,0:T(8,128)(2,1)S(1)}, bf16[64,8192]{1,0:T(8,128)(2,1)S(1)}, u32[]{:S(2)}, u32[]{:S(2)}) %collective-permute-start.24) | collective-permute-done | bytes 1048608 | tf_op jit(solution)/shard_map/ppermute | solution.py:38
  82.6 10.6 %collective-permute-done.25.refs_1_ = bf16[64,8192]{1,0:T(8,128)(2,1)S(1)} collective-permute-done((bf16[64,8192]{1,0:T(8,128)(2,1)S(1)}, bf16[64,8192]{1,0:T(8,128)(2,1)S(1)}, u32[]{:S(2)}, u32[]{:S(2)}) %collective-permute-start.25) | collective-permute-done | bytes 1048608 | tf_op jit(solution)/shard_map/ppermute | solution.py:38
  95.8 9.8 %project.5 = (bf16[512,512]{1,0:T(8,128)(2,1)S(1)}, bf16[512,256]{1,0:T(8,128)(2,1)S(1)}) custom-call(bf16[64,8192]{1,0:T(8,128)(2,1)S(1)} %collective-permute-done.9.refs_0_, bf16[64,8192]{1,0:T(8,128)(2,1)S(1)} %collective-permute-done.10.refs_1_, bf16[64,8192]{1,0:T(8,128)(2,1)S(1)} %collective-permute-done.11.refs_2_, ...), custom_call_target="tpu_custom_call" | custom-call | flops 6442450944 | bytes 20971520 | tf_op jit(solution)/shard_map/project/pallas_call | solution.py:109
  111.2 5.6 %collective-permute-done.20.refs_14_ = bf16[512,256]{1,0:T(8,128)(2,1)} collective-permute-done((bf16[512,256]{1,0:T(8,128)(2,1)S(1)}, bf16[512,256]{1,0:T(8,128)(2,1)}, u32[]{:S(2)}, u32[]{:S(2)}) %collective-permute-start.20) | collective-permute-done | bytes 262176 | tf_op jit(solution)/shard_map/ppermute | solution.py:46
  122.7 4.6 %copy-done.4 = bf16[8192,768]{1,0:T(8,128)(2,1)S(1)} copy-done((bf16[8192,768]{1,0:T(8,128)(2,1)S(1)}, bf16[8192,768]{1,0:T(8,128)(2,1)}, u32[]{:S(2)}) %copy-start.4) | copy-done | bytes 12582936
  127.3 5.6 %project.6.refs_16_ = bf16[256,256]{1,0:T(8,128)(2,1)S(1)} custom-call(bf16[64,8192]{1,0:T(8,128)(2,1)S(1)} %collective-permute-done.24.refs_0_, bf16[64,8192]{1,0:T(8,128)(2,1)S(1)} %collective-permute-done.25.refs_1_, bf16[64,8192]{1,0:T(8,128)(2,1)S(1)} %collective-permute-done.26.refs_2_, bf16[64,8192]{1,0:T(8,128)(2,1)} %collective-permute-done.27.refs_3_, ...), custom_call_target="tpu_custom_call" | custom-call | flops 1073741824 | bytes 8388608 | tf_op jit(solution)/shard_map/project/pallas_call | solution.py:109
  150.8 4.6 %copy-done.5 = bf16[8192,768]{1,0:T(8,128)(2,1)S(1)} copy-done((bf16[8192,768]{1,0:T(8,128)(2,1)S(1)}, bf16[8192,768]{1,0:T(8,128)(2,1)}, u32[]{:S(2)}) %copy-start.5) | copy-done | bytes 12582936
  155.4 6.5 %project.7.q_ref = bf16[256,512]{1,0:T(8,128)(2,1)S(1)} custom-call(bf16[64,8192]{1,0:T(8,128)(2,1)S(1)} %collective-permute-done.24.refs_0_, bf16[64,8192]{1,0:T(8,128)(2,1)S(1)} %collective-permute-done.25.refs_1_, bf16[64,8192]{1,0:T(8,128)(2,1)S(1)} %collective-permute-done.26.refs_2_, bf16[64,8192]{1,0:T(8,128)(2,1)} %collective-permute-done.27.refs_3_, ...), custom_call_target="tpu_custom_call" | custom-call | flops 2147483648 | bytes 12582912 | tf_op jit(solution)/shard_map/project/pallas_call | solution.py:109
  162.1 9.5 %attend.5 = (bf16[128,512]{1,0:T(8,128)(2,1)S(1)}, bf16[128,512]{1,0:T(8,128)(2,1)S(1)}) custom-call(s32[64]{0:T(128)S(1)} %fusion.4.table_ref, s32[16]{0:T(128)S(1)} %reduce.ends_ref, s32[2]{0:T(128)S(1)} %get-tuple-element.38.starts_ref, bf16[256,512]{1,0:T(8,128)(2,1)S(1)} %project.7.q_ref, bf16[256,256]{1,0:T(8,128)(2,1)S(1)} %copy-done.8, ...), custom_call_target="tpu_custom_call" | custom-call | flops 1073741824 | bytes 4718592 | tf_op jit(solution)/shard_map/attend/pallas_call | solution.py:213
  173.1 3.4 %copy-done = bf16[512,8192]{1,0:T(8,128)(2,1)S(1)} copy-done((bf16[512,8192]{1,0:T(8,128)(2,1)S(1)}, bf16[512,8192]{1,0:T(8,128)(2,1)}, u32[]{:S(2)}) %copy-start) | copy-done | bytes 8388632
  176.5 4.3 %out_project.11 = bf16[128,4096]{1,0:T(8,128)(2,1)S(1)} custom-call(bf16[128,512]{1,0:T(8,128)(2,1)S(1)} %get-tuple-element.30.own_ref, bf16[128,512]{1,0:T(8,128)(2,1)S(1)} %collective-permute-done.40.sib_ref, bf16[512,8192]{1,0:T(8,128)(2,1)S(1)} %copy-done, bf16[512,8192]{1,0:T(8,128)(2,1)} %collective-permute-done.36.w_sib), custom_call_target="tpu_custom_call" | custom-call | flops 1073741824 | bytes 9699328 | tf_op jit(solution)/shard_map/out_project/pallas_call | solution.py:240
  180.8 7.9 %collective-permute-start.43 = (bf16[128,4096]{1,0:T(8,128)(2,1)S(1)}, bf16[128,4096]{1,0:T(8,128)(2,1)}, u32[]{:S(2)}, u32[]{:S(2)}) collective-permute-start(bf16[128,4096]{1,0:T(8,128)(2,1)S(1)} %out_project.11), channel_id=1, source_target_pairs={{0,12},{2,14},{4,0},{6,2},{8,4},{10,6},{12,8},{14,10},{1,13},{3,15... | collective-permute-start | bytes 3145736 | tf_op jit(solution)/shard_map/ppermute | solution.py:38
  194.6 20.6 %attend.4 = (bf16[256,512]{1,0:T(8,128)(2,1)S(1)}, bf16[256,512]{1,0:T(8,128)(2,1)S(1)}) custom-call(s32[64]{0:T(128)S(1)} %fusion.4.table_ref, s32[16]{0:T(128)S(1)} %reduce.ends_ref, s32[4]{0:T(128)S(1)} %fusion.9.starts_ref, bf16[512,512]{1,0:T(8,128)(2,1)S(1)} %copy-done.52, bf16[256,256]{1,0:T(8,128)(2,1)S(1)} %copy-done.9, ...), custom_call_target="tpu_custom_call" | custom-call | flops 2147483648 | bytes 5242880 | tf_op jit(solution)/shard_map/attend/pallas_call | solution.py:213
  215.3 3.4 %copy-done.1 = bf16[512,8192]{1,0:T(8,128)(2,1)S(1)} copy-done((bf16[512,8192]{1,0:T(8,128)(2,1)S(1)}, bf16[512,8192]{1,0:T(8,128)(2,1)}, u32[]{:S(2)}) %copy-start.1) | copy-done | bytes 8388632
  218.7 4.2 %out_project.10 = bf16[128,4096]{1,0:T(8,128)(2,1)S(1)} custom-call(bf16[128,512]{1,0:T(8,128)(2,1)S(1)} %get-tuple-element.30.own_ref, bf16[128,512]{1,0:T(8,128)(2,1)S(1)} %collective-permute-done.40.sib_ref, bf16[512,8192]{1,0:T(8,128)(2,1)S(1)} %copy-done.1, bf16[512,8192]{1,0:T(8,128)(2,1)} %collective-permute-done.36.w_sib), custom_call_target="tpu_custom_call" | custom-call | flops 1073741824 | bytes 9699328 | tf_op jit(solution)/shard_map/out_project/pallas_call | solution.py:240
  223.0 5.2 %out_project.9 = (bf16[128,4096]{1,0:T(8,128)(2,1)S(1)}, bf16[128,4096]{1,0:T(8,128)(2,1)S(1)}) custom-call(bf16[256,512]{1,0:T(8,128)(2,1)S(1)} %get-tuple-element.25.own_ref, bf16[256,512]{1,0:T(8,128)(2,1)S(1)} %collective-permute-done.37.sib_ref, bf16[512,8192]{1,0:T(8,128)(2,1)S(1)} %copy-done.1, bf16[512,8192]{1,0:T(8,128)(2,1)} %collective-permute-done.36.w_sib), custom_call_target="tpu_custom_call" | custom-call | flops 2147483648 | bytes 11010048 | tf_op jit(solution)/shard_map/out_project/pallas_call | solution.py:240
  228.2 5.1 %out_project.8 = (bf16[128,4096]{1,0:T(8,128)(2,1)S(1)}, bf16[128,4096]{1,0:T(8,128)(2,1)S(1)}) custom-call(bf16[256,512]{1,0:T(8,128)(2,1)S(1)} %get-tuple-element.25.own_ref, bf16[256,512]{1,0:T(8,128)(2,1)S(1)} %collective-permute-done.37.sib_ref, bf16[512,8192]{1,0:T(8,128)(2,1)S(1)} %copy-done.1, bf16[512,8192]{1,0:T(8,128)(2,1)} %collective-permute-done.36.w_sib), custom_call_target="tpu_custom_call" | custom-call | flops 2147483648 | bytes 11010048 | tf_op jit(solution)/shard_map/out_project/pallas_call | solution.py:240
  233.4 3.3 %collective-permute-start.38 = (bf16[128,4096]{1,0:T(8,128)(2,1)S(1)}, bf16[128,4096]{1,0:T(8,128)(2,1)S(1)}, u32[]{:S(2)}, u32[]{:S(2)}) collective-permute-start(bf16[128,4096]{1,0:T(8,128)(2,1)S(1)} %get-tuple-element.27), channel_id=1, source_target_pairs={{0,12},{2,14},{4,0},{6,2},{8,4},{10,6},{12,8},{14,10},{1,13},{3,15... | collective-permute-start | bytes 3145736 | tf_op jit(solution)/shard_map/ppermute | solution.py:38
  240.4 9.7 %collective-permute-done.41 = bf16[128,4096]{1,0:T(8,128)(2,1)S(1)} collective-permute-done((bf16[128,4096]{1,0:T(8,128)(2,1)S(1)}, bf16[128,4096]{1,0:T(8,128)(2,1)S(1)}, u32[]{:S(2)}, u32[]{:S(2)}) %collective-permute-start.41) | collective-permute-done | bytes 1048608 | tf_op jit(solution)/shard_map/ppermute | solution.py:38
  250.5 12.9 %attend.3 = (bf16[128,512]{1,0:T(8,128)(2,1)S(1)}, bf16[128,512]{1,0:T(8,128)(2,1)S(1)}) custom-call(s32[64]{0:T(128)S(1)} %fusion.4.table_ref, s32[16]{0:T(128)S(1)} %reduce.ends_ref, s32[2]{0:T(128)S(1)} %get-tuple-element.37.starts_ref, bf16[256,512]{1,0:T(8,128)(2,1)S(1)} %copy-done.48, bf16[256,256]{1,0:T(8,128)(2,1)S(1)} %copy-done.10, ...), custom_call_target="tpu_custom_call" | custom-call | flops 1073741824 | bytes 4718592 | tf_op jit(solution)/shard_map/attend/pallas_call | solution.py:213
  264.8 4.2 %out_project.7.p_hi = bf16[128,4096]{1,0:T(8,128)(2,1)S(1)} custom-call(bf16[128,512]{1,0:T(8,128)(2,1)S(1)} %get-tuple-element.22.own_ref, bf16[128,512]{1,0:T(8,128)(2,1)S(1)} %collective-permute-done.35.sib_ref, bf16[512,8192]{1,0:T(8,128)(2,1)S(1)} %bitcast.13, bf16[512,8192]{1,0:T(8,128)(2,1)} %collective-permute-done.36.w_sib), custom_call_target="tpu_custom_call" | custom-call | flops 1073741824 | bytes 9699328 | tf_op jit(solution)/shard_map/out_project/pallas_call | solution.py:240
  269.0 4.2 %out_project.6.p_lo = bf16[128,4096]{1,0:T(8,128)(2,1)S(1)} custom-call(bf16[128,512]{1,0:T(8,128)(2,1)S(1)} %get-tuple-element.22.own_ref, bf16[128,512]{1,0:T(8,128)(2,1)S(1)} %collective-permute-done.35.sib_ref, bf16[512,8192]{1,0:T(8,128)(2,1)S(1)} %bitcast.13, bf16[512,8192]{1,0:T(8,128)(2,1)} %collective-permute-done.36.w_sib), custom_call_target="tpu_custom_call" | custom-call | flops 1073741824 | bytes 9699328 | tf_op jit(solution)/shard_map/out_project/pallas_call | solution.py:240
  273.2 8.7 %collective-permute-done.44.b_hi = bf16[128,4096]{1,0:T(8,128)(2,1)S(1)} collective-permute-done((bf16[128,4096]{1,0:T(8,128)(2,1)S(1)}, bf16[128,4096]{1,0:T(8,128)(2,1)S(1)}, u32[]{:S(2)}, u32[]{:S(2)}) %collective-permute-start.44) | collective-permute-done | bytes 1048608 | tf_op jit(solution)/shard_map/ppermute | solution.py:38
  281.9 12.7 %collective-permute-done.42.b_lo = bf16[128,4096]{1,0:T(8,128)(2,1)S(1)} collective-permute-done((bf16[128,4096]{1,0:T(8,128)(2,1)S(1)}, bf16[128,4096]{1,0:T(8,128)(2,1)S(1)}, u32[]{:S(2)}, u32[]{:S(2)}) %collective-permute-start.42) | collective-permute-done | bytes 1048608 | tf_op jit(solution)/shard_map/ppermute | solution.py:38
  (205 shorter events, 60.7 us)
Async XLA Ops:
  0.0 173.0 %collective-permute-start.36 = (bf16[512,8192]{1,0:T(8,128)(2,1)}, bf16[512,8192]{1,0:T(8,128)(2,1)}, u32[]{:S(2)}, u32[]{:S(2)}) collective-permute-start(bf16[512,8192]{1,0:T(8,128)(2,1)} %w_own.11), channel_id=1, source_target_pairs={{0,2},{2,0},{4,6},{6,4},{8,10},{10,8},{12,14},{14,12},{1,3},{3,1},... | collective-permute-start | bytes 25165832 | tf_op jit(solution)/shard_map/ppermute | solution.py:42
  3.0 27.2 %collective-permute-start.13 = (bf16[64,8192]{1,0:T(8,128)(2,1)S(1)}, bf16[64,8192]{1,0:T(8,128)(2,1)S(1)}, u32[]{:S(2)}, u32[]{:S(2)}) collective-permute-start(bf16[64,8192]{1,0:T(8,128)(2,1)S(1)} %norm_piece.2.refs_0_), channel_id=1, source_target_pairs={{0,12},{2,14},{4,0},{6,2},{8,4},{10,6},{12,8},{14,10},{1,13},{3,15... | collective-permute-start | bytes 3145736 | tf_op jit(solution)/shard_map/ppermute | solution.py:38
  7.1 26.8 %collective-permute-start.9 = (bf16[64,8192]{1,0:T(8,128)(2,1)S(1)}, bf16[64,8192]{1,0:T(8,128)(2,1)S(1)}, u32[]{:S(2)}, u32[]{:S(2)}) collective-permute-start(bf16[64,8192]{1,0:T(8,128)(2,1)S(1)} %norm_piece.2.refs_0_), channel_id=1, source_target_pairs={{0,4},{2,6},{4,8},{6,10},{8,12},{10,14},{12,0},{14,2},{1,5},{3,7},... | collective-permute-start | bytes 3145736 | tf_op jit(solution)/shard_map/ppermute | solution.py:38
  7.1 26.8 %collective-permute-start = (bf16[64,8192]{1,0:T(8,128)(2,1)S(1)}, bf16[64,8192]{1,0:T(8,128)(2,1)S(1)}, u32[]{:S(2)}, u32[]{:S(2)}) collective-permute-start(bf16[64,8192]{1,0:T(8,128)(2,1)S(1)} %norm_piece.2.refs_0_), channel_id=1, source_target_pairs={{0,2},{2,0},{4,6},{6,4},{8,10},{10,8},{12,14},{14,12},{1,3},{3,1},... | collective-permute-start | bytes 3145736 | tf_op jit(solution)/shard_map/ppermute | solution.py:42
  8.0 26.0 %collective-permute-start.1 = (bf16[64,8192]{1,0:T(8,128)(2,1)S(1)}, bf16[64,8192]{1,0:T(8,128)(2,1)S(1)}, u32[]{:S(2)}, u32[]{:S(2)}) collective-permute-start(bf16[64,8192]{1,0:T(8,128)(2,1)S(1)} %norm_piece.3.refs_1_), channel_id=1, source_target_pairs={{0,2},{2,0},{4,6},{6,4},{8,10},{10,8},{12,14},{14,12},{1,3},{3,1},... | collective-permute-start | bytes 3145736 | tf_op jit(solution)/shard_map/ppermute | solution.py:42
  30.2 26.0 %collective-permute-start.14 = (bf16[64,8192]{1,0:T(8,128)(2,1)S(1)}, bf16[64,8192]{1,0:T(8,128)(2,1)S(1)}, u32[]{:S(2)}, u32[]{:S(2)}) collective-permute-start(bf16[64,8192]{1,0:T(8,128)(2,1)S(1)} %norm_piece.3.refs_1_), channel_id=1, source_target_pairs={{0,12},{2,14},{4,0},{6,2},{8,4},{10,6},{12,8},{14,10},{1,13},{3,15... | collective-permute-start | bytes 3145736 | tf_op jit(solution)/shard_map/ppermute | solution.py:38
  33.9 27.3 %collective-permute-start.10 = (bf16[64,8192]{1,0:T(8,128)(2,1)S(1)}, bf16[64,8192]{1,0:T(8,128)(2,1)S(1)}, u32[]{:S(2)}, u32[]{:S(2)}) collective-permute-start(bf16[64,8192]{1,0:T(8,128)(2,1)S(1)} %norm_piece.3.refs_1_), channel_id=1, source_target_pairs={{0,4},{2,6},{4,8},{6,10},{8,12},{10,14},{12,0},{14,2},{1,5},{3,7},... | collective-permute-start | bytes 3145736 | tf_op jit(solution)/shard_map/ppermute | solution.py:38
  33.9 37.4 %collective-permute-start.15 = (bf16[64,8192]{1,0:T(8,128)(2,1)S(1)}, bf16[64,8192]{1,0:T(8,128)(2,1)S(1)}, u32[]{:S(2)}, u32[]{:S(2)}) collective-permute-start(bf16[64,8192]{1,0:T(8,128)(2,1)S(1)} %collective-permute-done.13.refs_4_), channel_id=1, source_target_pairs={{0,2},{2,0},{4,6},{6,4},{8,10},{10,8},{12,14},{14,12},{1,3},{3,1},... | collective-permute-start | bytes 3145736 | tf_op jit(solution)/shard_map/ppermute | solution.py:42
  34.0 48.1 %collective-permute-start.24 = (bf16[64,8192]{1,0:T(8,128)(2,1)S(1)}, bf16[64,8192]{1,0:T(8,128)(2,1)S(1)}, u32[]{:S(2)}, u32[]{:S(2)}) collective-permute-start(bf16[64,8192]{1,0:T(8,128)(2,1)S(1)} %collective-permute-done.9.refs_0_), channel_id=1, source_target_pairs={{0,4},{2,6},{4,8},{6,10},{8,12},{10,14},{12,0},{14,2},{1,5},{3,7},... | collective-permute-start | bytes 3145736 | tf_op jit(solution)/shard_map/ppermute | solution.py:38
  67.7 14.4 %collective-permute-start.11 = (bf16[64,8192]{1,0:T(8,128)(2,1)S(1)}, bf16[64,8192]{1,0:T(8,128)(2,1)S(1)}, u32[]{:S(2)}, u32[]{:S(2)}) collective-permute-start(bf16[64,8192]{1,0:T(8,128)(2,1)S(1)} %collective-permute-done.9.refs_0_), channel_id=1, source_target_pairs={{0,2},{2,0},{4,6},{6,4},{8,10},{10,8},{12,14},{14,12},{1,3},{3,1},... | collective-permute-start | bytes 3145736 | tf_op jit(solution)/shard_map/ppermute | solution.py:42
  71.2 22.1 %collective-permute-start.25 = (bf16[64,8192]{1,0:T(8,128)(2,1)S(1)}, bf16[64,8192]{1,0:T(8,128)(2,1)S(1)}, u32[]{:S(2)}, u32[]{:S(2)}) collective-permute-start(bf16[64,8192]{1,0:T(8,128)(2,1)S(1)} %collective-permute-done.14.refs_5_), channel_id=1, source_target_pairs={{0,12},{2,14},{4,0},{6,2},{8,4},{10,6},{12,8},{14,10},{1,13},{3,15... | collective-permute-start | bytes 3145736 | tf_op jit(solution)/shard_map/ppermute | solution.py:38
  71.3 24.3 %collective-permute-start.16 = (bf16[64,8192]{1,0:T(8,128)(2,1)S(1)}, bf16[64,8192]{1,0:T(8,128)(2,1)S(1)}, u32[]{:S(2)}, u32[]{:S(2)}) collective-permute-start(bf16[64,8192]{1,0:T(8,128)(2,1)S(1)} %collective-permute-done.14.refs_5_), channel_id=1, source_target_pairs={{0,2},{2,0},{4,6},{6,4},{8,10},{10,8},{12,14},{14,12},{1,3},{3,1},... | collective-permute-start | bytes 3145736 | tf_op jit(solution)/shard_map/ppermute | solution.py:42
  82.1 13.6 %collective-permute-start.12 = (bf16[64,8192]{1,0:T(8,128)(2,1)S(1)}, bf16[64,8192]{1,0:T(8,128)(2,1)S(1)}, u32[]{:S(2)}, u32[]{:S(2)}) collective-permute-start(bf16[64,8192]{1,0:T(8,128)(2,1)S(1)} %collective-permute-done.10.refs_1_), channel_id=1, source_target_pairs={{0,2},{2,0},{4,6},{6,4},{8,10},{10,8},{12,14},{14,12},{1,3},{3,1},... | collective-permute-start | bytes 3145736 | tf_op jit(solution)/shard_map/ppermute | solution.py:42
  82.1 37.6 %collective-permute-start.26 = (bf16[64,8192]{1,0:T(8,128)(2,1)S(1)}, bf16[64,8192]{1,0:T(8,128)(2,1)S(1)}, u32[]{:S(2)}, u32[]{:S(2)}) collective-permute-start(bf16[64,8192]{1,0:T(8,128)(2,1)S(1)} %collective-permute-done.24.refs_0_), channel_id=1, source_target_pairs={{0,2},{2,0},{4,6},{6,4},{8,10},{10,8},{12,14},{14,12},{1,3},{3,1},... | collective-permute-start | bytes 3145736 | tf_op jit(solution)/shard_map/ppermute | solution.py:42
  93.3 13.2 %collective-permute-start.8 = (bf16[256,256]{1,0:T(8,128)(2,1)S(1)}, bf16[256,256]{1,0:T(8,128)(2,1)S(1)}, u32[]{:S(2)}, u32[]{:S(2)}) collective-permute-start(bf16[256,256]{1,0:T(8,128)(2,1)S(1)} %collective-permute-done.2.refs_1_), channel_id=1, source_target_pairs={{0,32},{16,48},{32,64},{48,80},{64,96},{80,112},{96,0},{112,16},{1... | collective-permute-start | bytes 393224 | tf_op jit(solution)/shard_map/ppermute | solution.py:46
  95.7 13.4 %collective-permute-start.4 = (bf16[256,256]{1,0:T(8,128)(2,1)S(1)}, bf16[256,256]{1,0:T(8,128)(2,1)S(1)}, u32[]{:S(2)}, u32[]{:S(2)}) collective-permute-start(bf16[256,256]{1,0:T(8,128)(2,1)S(1)} %collective-permute-done.2.refs_1_), channel_id=1, source_target_pairs={{0,96},{16,112},{32,0},{48,16},{64,32},{80,48},{96,64},{112,80},{1... | collective-permute-start | bytes 393224 | tf_op jit(solution)/shard_map/ppermute | solution.py:46
  95.7 26.8 %collective-permute-start.27 = (bf16[64,8192]{1,0:T(8,128)(2,1)S(1)}, bf16[64,8192]{1,0:T(8,128)(2,1)}, u32[]{:S(2)}, u32[]{:S(2)}) collective-permute-start(bf16[64,8192]{1,0:T(8,128)(2,1)S(1)} %collective-permute-done.25.refs_1_), channel_id=1, source_target_pairs={{0,2},{2,0},{4,6},{6,4},{8,10},{10,8},{12,14},{14,12},{1,3},{3,1},... | collective-permute-start | bytes 3145736 | tf_op jit(solution)/shard_map/ppermute | solution.py:42
  116.8 16.1 %collective-permute-start.7 = (bf16[256,256]{1,0:T(8,128)(2,1)}, bf16[256,256]{1,0:T(8,128)(2,1)}, u32[]{:S(2)}, u32[]{:S(2)}) collective-permute-start(bf16[256,256]{1,0:T(8,128)(2,1)} %copy-done.31), channel_id=1, source_target_pairs={{0,96},{16,112},{32,0},{48,16},{64,32},{80,48},{96,64},{112,80},{1... | collective-permute-start | bytes 393224 | tf_op jit(solution)/shard_map/ppermute | solution.py:46
  119.7 16.7 %collective-permute-start.18 = (bf16[512,256]{1,0:T(8,128)(2,1)S(1)}, bf16[512,256]{1,0:T(8,128)(2,1)}, u32[]{:S(2)}, u32[]{:S(2)}) collective-permute-start(bf16[512,256]{1,0:T(8,128)(2,1)S(1)} %get-tuple-element.21.refs_8_), channel_id=1, source_target_pairs={{0,96},{16,112},{32,0},{48,16},{64,32},{80,48},{96,64},{112,80},{1... | collective-permute-start | bytes 786440 | tf_op jit(solution)/shard_map/ppermute | solution.py:46
  119.7 14.9 %collective-permute-start.19 = (bf16[512,256]{1,0:T(8,128)(2,1)}, bf16[512,256]{1,0:T(8,128)(2,1)}, u32[]{:S(2)}, u32[]{:S(2)}) collective-permute-start(bf16[512,256]{1,0:T(8,128)(2,1)} %collective-permute-done.17.refs_9_), channel_id=1, source_target_pairs={{0,96},{16,112},{32,0},{48,16},{64,32},{80,48},{96,64},{112,80},{1... | collective-permute-start | bytes 786440 | tf_op jit(solution)/shard_map/ppermute | solution.py:46
  122.5 16.0 %collective-permute-start.21 = (bf16[512,256]{1,0:T(8,128)(2,1)}, bf16[512,256]{1,0:T(8,128)(2,1)}, u32[]{:S(2)}, u32[]{:S(2)}) collective-permute-start(bf16[512,256]{1,0:T(8,128)(2,1)} %collective-permute-done.20.refs_14_), channel_id=1, source_target_pairs={{0,32},{16,48},{32,64},{48,80},{64,96},{80,112},{96,0},{112,16},{1... | collective-permute-start | bytes 786440 | tf_op jit(solution)/shard_map/ppermute | solution.py:46
  132.9 13.8 %collective-permute-start.23 = (bf16[512,256]{1,0:T(8,128)(2,1)}, bf16[512,256]{1,0:T(8,128)(2,1)}, u32[]{:S(2)}, u32[]{:S(2)}) collective-permute-start(bf16[512,256]{1,0:T(8,128)(2,1)} %collective-permute-done.17.refs_9_), channel_id=1, source_target_pairs={{0,32},{16,48},{32,64},{48,80},{64,96},{80,112},{96,0},{112,16},{1... | collective-permute-start | bytes 786440 | tf_op jit(solution)/shard_map/ppermute | solution.py:46
  146.7 15.3 %collective-permute-start.29 = (bf16[256,256]{1,0:T(8,128)(2,1)S(1)}, bf16[256,256]{1,0:T(8,128)(2,1)S(1)}, u32[]{:S(2)}, u32[]{:S(2)}) collective-permute-start(bf16[256,256]{1,0:T(8,128)(2,1)S(1)} %project.6.refs_16_), channel_id=1, source_target_pairs={{0,96},{16,112},{32,0},{48,16},{64,32},{80,48},{96,64},{112,80},{1... | collective-permute-start | bytes 393224 | tf_op jit(solution)/shard_map/ppermute | solution.py:46
  146.9 15.0 %collective-permute-start.34 = (bf16[256,256]{1,0:T(8,128)(2,1)}, bf16[256,256]{1,0:T(8,128)(2,1)S(1)}, u32[]{:S(2)}, u32[]{:S(2)}) collective-permute-start(bf16[256,256]{1,0:T(8,128)(2,1)} %collective-permute-done.28.refs_17_), channel_id=1, source_target_pairs={{0,32},{16,48},{32,64},{48,80},{64,96},{80,112},{96,0},{112,16},{1... | collective-permute-start | bytes 393224 | tf_op jit(solution)/shard_map/ppermute | solution.py:46
  148.8 13.2 %collective-permute-start.32 = (bf16[256,256]{1,0:T(8,128)(2,1)}, bf16[256,256]{1,0:T(8,128)(2,1)S(1)}, u32[]{:S(2)}, u32[]{:S(2)}) collective-permute-start(bf16[256,256]{1,0:T(8,128)(2,1)} %collective-permute-done.31.refs_22_), channel_id=1, source_target_pairs={{0,32},{16,48},{32,64},{48,80},{64,96},{80,112},{96,0},{112,16},{1... | collective-permute-start | bytes 393224 | tf_op jit(solution)/shard_map/ppermute | solution.py:46
  149.0 13.0 %collective-permute-start.33 = (bf16[256,256]{1,0:T(8,128)(2,1)}, bf16[256,256]{1,0:T(8,128)(2,1)S(1)}, u32[]{:S(2)}, u32[]{:S(2)}) collective-permute-start(bf16[256,256]{1,0:T(8,128)(2,1)} %collective-permute-done.30.refs_19_), channel_id=1, source_target_pairs={{0,96},{16,112},{32,0},{48,16},{64,32},{80,48},{96,64},{112,80},{1... | collective-permute-start | bytes 393224 | tf_op jit(solution)/shard_map/ppermute | solution.py:46
  180.8 55.8 %collective-permute-start.43 = (bf16[128,4096]{1,0:T(8,128)(2,1)S(1)}, bf16[128,4096]{1,0:T(8,128)(2,1)}, u32[]{:S(2)}, u32[]{:S(2)}) collective-permute-start(bf16[128,4096]{1,0:T(8,128)(2,1)S(1)} %out_project.11), channel_id=1, source_target_pairs={{0,12},{2,14},{4,0},{6,2},{8,4},{10,6},{12,8},{14,10},{1,13},{3,15... | collective-permute-start | bytes 3145736 | tf_op jit(solution)/shard_map/ppermute | solution.py:38
  222.9 27.2 %collective-permute-start.41 = (bf16[128,4096]{1,0:T(8,128)(2,1)S(1)}, bf16[128,4096]{1,0:T(8,128)(2,1)S(1)}, u32[]{:S(2)}, u32[]{:S(2)}) collective-permute-start(bf16[128,4096]{1,0:T(8,128)(2,1)S(1)} %out_project.10), channel_id=1, source_target_pairs={{0,4},{2,6},{4,8},{6,10},{8,12},{10,14},{12,0},{14,2},{1,5},{3,7},... | collective-permute-start | bytes 3145736 | tf_op jit(solution)/shard_map/ppermute | solution.py:38
  228.1 45.1 %collective-permute-start.39 = (bf16[128,4096]{1,0:T(8,128)(2,1)S(1)}, bf16[128,4096]{1,0:T(8,128)(2,1)S(1)}, u32[]{:S(2)}, u32[]{:S(2)}) collective-permute-start(bf16[128,4096]{1,0:T(8,128)(2,1)S(1)} %get-tuple-element.28), channel_id=1, source_target_pairs={{0,4},{2,6},{4,8},{6,10},{8,12},{10,14},{12,0},{14,2},{1,5},{3,7},... | collective-permute-start | bytes 3145736 | tf_op jit(solution)/shard_map/ppermute | solution.py:38
  233.4 39.8 %collective-permute-start.38 = (bf16[128,4096]{1,0:T(8,128)(2,1)S(1)}, bf16[128,4096]{1,0:T(8,128)(2,1)S(1)}, u32[]{:S(2)}, u32[]{:S(2)}) collective-permute-start(bf16[128,4096]{1,0:T(8,128)(2,1)S(1)} %get-tuple-element.27), channel_id=1, source_target_pairs={{0,12},{2,14},{4,0},{6,2},{8,4},{10,6},{12,8},{14,10},{1,13},{3,15... | collective-permute-start | bytes 3145736 | tf_op jit(solution)/shard_map/ppermute | solution.py:38
  238.2 43.7 %collective-permute-start.44 = (bf16[128,4096]{1,0:T(8,128)(2,1)S(1)}, bf16[128,4096]{1,0:T(8,128)(2,1)S(1)}, u32[]{:S(2)}, u32[]{:S(2)}) collective-permute-start(bf16[128,4096]{1,0:T(8,128)(2,1)S(1)} %add_convert_fusion), channel_id=1, source_target_pairs={{0,12},{2,14},{4,0},{6,2},{8,4},{10,6},{12,8},{14,10},{1,13},{3,15... | collective-permute-start | bytes 3145736 | tf_op jit(solution)/shard_map/ppermute | solution.py:38
  250.3 44.3 %collective-permute-start.42 = (bf16[128,4096]{1,0:T(8,128)(2,1)S(1)}, bf16[128,4096]{1,0:T(8,128)(2,1)S(1)}, u32[]{:S(2)}, u32[]{:S(2)}) collective-permute-start(bf16[128,4096]{1,0:T(8,128)(2,1)S(1)} %add_convert_fusion.1), channel_id=1, source_target_pairs={{0,4},{2,6},{4,8},{6,10},{8,12},{10,14},{12,0},{14,2},{1,5},{3,7},... | collective-permute-start | bytes 3145736 | tf_op jit(solution)/shard_map/ppermute | solution.py:38
  (70 other events, 878.1 us)
